TPU v7x, 32 devices: a whole 2x2x4 slice. The times are simulated.
32 devices in a mesh: draws: 2 (over y), dst: 4 (over z), org: 2 (over x), st: 2 (over core).
Axes of the slice: x: 2, y: 2, z: 4, core: 2. Of those that a mesh axis runs over, the one named last changes fastest.
Arguments:
- value_now: float32 [8, 2, 64, 4096], P(('draws', 'dst'), 'org', None, 'st'), parts along dimension 0, may hold values from -90 to 490
- utility: float32 [8, 2, 64, 4096], P(('draws', 'dst'), 'org', None, 'st'), parts along dimension 0, may hold values from -6 to 6
- move_costs: float32 [8, 2, 64, 4, 128], P('draws', 'org', None, 'dst'), parts along dimension 0, may hold values from 0 to 3
- dest_blocks: int32 [8, 3], replicated, may hold values from 0 to 7, all different within a row
- row_counts: int32 [8], replicated, may hold values from 1 to 3, as said below
- transition: int32 [4096], replicated, may hold values from 0 to 4095
Outputs:
- value_next: float32 [8, 2, 64, 4096], P(('draws', 'dst'), 'org', None, 'st'), parts along dimension 0
There are 2 independent parts, one for each index of `draws`. A program takes and returns all parts, laid end to end along the dimension named above; an argument that names none is the same for every part. Nothing has to cross between parts.
Inputs may be any that keep to these rules, and one draw needn't show every extreme that they name: `dest_blocks`: each row names 3 different blocks; only the first row_counts[o] of row o count. `row_counts`: some anchor block has 3.
All inputs are finite; a program needn't handle non-finite values.
Results may differ from a plain program's by a relative error of at most 0.00095.
Values may be sent and summed in bfloat16 or wider, within the bound.
No kernel may reach another device: no remote copies, remote signals or barrier semaphores. Data moves between devices by JAX's collectives and lax.ppermute only.
A program may use at most 64 MiB of HBM per device.

v0:
```python
import functools

import jax
import jax.numpy as jnp
from jax import lax
from jax.experimental import pallas as pl
from jax.experimental.pallas import tpu as pltpu
from jax.sharding import PartitionSpec as P


DISCOUNT = 0.95
FLOOR = -1e30
LANES = 128
CHUNKS = 2
LOW_BITS = 8
GRANT = 24 * 2**20
TILES = 4


def call(kernel, outs, flops, touched, args, smem=(), fetched=()):
    specs = [pl.BlockSpec(memory_space=pltpu.SMEM if n in smem else pltpu.VMEM) for n in range(len(args))]
    specs = [pl.BlockSpec() if n in fetched else spec for n, spec in enumerate(specs)]
    spaces = {n: pltpu.HBM for n in fetched}
    held = [
        a if n in smem else pltpu.with_memory_space_constraint(a, spaces.get(n, pltpu.VMEM)) for n, a in enumerate(args)
    ]
    return pl.pallas_call(
        kernel,
        in_specs=specs,
        out_specs=[pl.BlockSpec(memory_space=pltpu.VMEM)] * len(outs),
        out_shape=[pltpu.VMEM(shape, dtype) for shape, dtype in outs],
        compiler_params=pltpu.CompilerParams(vmem_limit_bytes=GRANT),
        cost_estimate=pl.CostEstimate(flops=flops, bytes_accessed=touched, transcendentals=0),
    )(*held)


def put(ref, at, value):
    rows = value.shape[0]
    for n in range(value.shape[1] // LANES):
        ref[at + n * rows : at + (n + 1) * rows, :] = value[:, n * LANES : (n + 1) * LANES]
    return at + value.shape[1] // LANES * rows


def get(ref, at, rows, width):
    parts = [ref[at + n * rows : at + (n + 1) * rows, :] for n in range(width // LANES)]
    return jnp.concatenate(parts, axis=1)


def rows_to_lanes(block, first, count):
    return jnp.concatenate([block[first + i : first + i + 1, :] for i in range(count)], axis=1)


def lanes_to_rows(row):
    return jnp.concatenate([row[:, i : i + LANES] for i in range(0, row.shape[1], LANES)], axis=0)


def place(low):
    d = lax.axis_index("dst")
    return d // low, d % low


def weigh_kernel(high, low, orig, widths, value_ref, cost_ref, *out_refs):
    plain_refs, keyed_refs, own_ref = out_refs[: len(widths)], out_refs[len(widths) : -1], out_refs[-1]
    my_high, my_low = place(low)
    my_orig = lax.axis_index("org")
    rows = value_ref.shape[0]
    cols = cost_ref.shape[2]

    def kernel_part(turn):
        target = (my_low + low - turn) % low
        parts = []
        for r in range(high):
            k = jnp.exp(-cost_ref[((my_high + r) % high) * low + target])
            turned = k
            for s in range(1, orig):
                turned = jnp.where(my_orig == s, pltpu.roll(k, cols - s * rows, 1), turned)
            parts.append(turned.astype(jnp.bfloat16))
        return parts

    at = 0
    for part in kernel_part(0):
        at = put(own_ref, at, part)
    for turn in range(1, low):
        at = 0
        for part in kernel_part(turn):
            at = put(keyed_refs[turn - 1], at, part)
    start = 0
    tops = []
    for c, width in enumerate(widths):
        v = value_ref[:, start : start + width]
        top = jnp.max(v, axis=0, keepdims=True).astype(jnp.bfloat16).astype(jnp.float32)
        tops.append(top)
        e = jnp.exp(v - top).astype(jnp.bfloat16)
        end = put(plain_refs[c], 0, e)
        if c == 0:
            first = end
            for ref in keyed_refs:
                put(ref, own_ref.shape[0], e)
        start += width
    packed = lanes_to_rows(jnp.concatenate(tops, axis=1)).astype(jnp.bfloat16)
    plain_refs[0][first:, :] = packed
    for ref in keyed_refs:
        ref[own_ref.shape[0] + first :, :] = packed


def weigh(high, low, orig, widths, value, cost):
    rows, states = value.shape
    tops = states // LANES
    keys = high * rows * cost.shape[2] // LANES
    sizes = [rows * w // LANES + (tops if c == 0 else 0) for c, w in enumerate(widths)]
    sizes += [keys + sizes[0]] * (low - 1) + [keys]
    outs = [((size, LANES), jnp.bfloat16) for size in sizes]
    kernel = functools.partial(weigh_kernel, high, low, orig, widths)
    return call(kernel, outs, 8 * rows * states, 8 * rows * states, (value, cost), fetched=(0, 1))


def sums_kernel(low, orig, rows, chunk, widths, turns, open_ref, own_ref, *refs):
    groups = low * orig
    width = widths[chunk]
    first = sum(widths[:chunk]) // LANES
    keys = own_ref.shape[0]
    skips = [keys if b >= orig and b % orig == 0 else 0 for b in range(groups)]
    ends = [skip + rows * widths[0] // LANES for skip in skips]
    tops = [refs[b][ends[b] :, :].astype(jnp.float32) for b in range(groups)]
    pieces = refs[:groups] if chunk == 0 else refs[groups : 2 * groups]
    out_refs = refs[-len(turns) :]
    for n, turn in enumerate(turns):
        feasible = [open_ref[turn * groups + b : turn * groups + b + 1, :] > 0.5 for b in range(groups)]
        ceiling = functools.reduce(jnp.maximum, [jnp.where(f, t, FLOOR) for f, t in zip(feasible, tops)])
        total = jnp.zeros((rows, width), jnp.float32)
        for i in range(low):
            key_ref = own_ref if i == 0 else refs[i * orig]
            for j in range(orig):
                b = i * orig + j
                scale = jnp.exp(jnp.where(feasible[b], tops[b] - ceiling, FLOOR))
                column = (turn * orig + j) * rows
                at, column = column // LANES * rows, column % LANES
                product = jnp.dot(
                    key_ref[at : at + rows, column : column + rows],
                    get(pieces[b], skips[b] if chunk == 0 else 0, rows, width),
                    preferred_element_type=jnp.float32,
                )
                total += rows_to_lanes(scale, first, width // LANES) * product
        end = put(out_refs[n], 0, total.astype(jnp.bfloat16))
        if chunk == 0:
            out_refs[n][end:, :] = ceiling.astype(jnp.bfloat16)


def sums(low, orig, rows, chunk, widths, turns, open_to, own_key, gathered):
    width = widths[chunk]
    groups = low * orig
    args = [open_to, own_key, *gathered[0]]
    if chunk > 0:
        args += gathered[chunk]
    size = rows * width // LANES + (sum(widths) // LANES if chunk == 0 else 0)
    outs = [((size, LANES), jnp.bfloat16)] * len(turns)
    kernel = functools.partial(sums_kernel, low, orig, rows, chunk, widths, turns)
    flops = 2 * rows * rows * width * groups * len(turns)
    return call(kernel, outs, flops, 2 * rows * width * (groups + len(turns)), args)


def spot_kernel(high, low, orig, transition_ref, count_ref, list_ref, high_ref, onehot_ref, open_ref):
    nxt = transition_ref[pl.ds(lax.axis_index("st"), 1), :]
    high_ref[...] = lax.shift_right_logical(nxt, LOW_BITS)
    low_part = nxt & (onehot_ref.shape[0] - 1)
    rows = lax.broadcasted_iota(jnp.int32, onehot_ref.shape, 0)
    onehot_ref[...] = jnp.where(rows == low_part, 1.0, 0.0).astype(jnp.bfloat16)
    slots = list_ref.shape[1]
    my_high, my_low = place(low)
    my_orig = lax.axis_index("org")
    for turn in range(high):
        anchor = (((my_high + turn) % high) * low + my_low) * orig + my_orig
        limit = count_ref[anchor]
        for i in range(low):
            for j in range(orig):
                block = (my_high * low + (my_low + i) % low) * orig + (my_orig + j) % orig

                def hit(k, found):
                    return found | jnp.where((list_ref[anchor, k] == block) & (k < limit), 1, 0)

                found = lax.fori_loop(0, slots, hit, jnp.int32(0), unroll=slots <= 4)
                at = (turn * low + i) * orig + j
                open_ref[at : at + 1, :] = jnp.full((1, LANES), found.astype(jnp.float32))


def spot(high, low, orig, halves, transition, row_counts, dest_blocks):
    states = transition.shape[0] // halves
    size = 2**LOW_BITS
    outs = [
        ((1, states), jnp.int32),
        ((size, states), jnp.bfloat16),
        ((-(-high * low * orig // 8) * 8, LANES), jnp.float32),
    ]
    args = (transition.reshape(halves, states), row_counts, dest_blocks)
    kernel = functools.partial(spot_kernel, high, low, orig)
    return call(kernel, outs, 4 * size * states, 2 * size * states, args, smem=(1, 2))


def pick(halves, cores, widths, chunk, where, onehot, states, got, value):
    size = onehot.shape[0]
    rows = value.shape[0]
    mine = lax.axis_index("st")
    start = sum(widths[:chunk]) // size
    stack, parts = [], []
    for h, ref in zip(cores, got):
        part = ((mine + h) % halves) * (states // size) + start
        for k in range(widths[chunk] // size):
            stack.append(get(ref, k * size // LANES * rows, rows, size))
            parts.append(part + k)
    every = jnp.dot(jnp.concatenate(stack, axis=0), onehot, preferred_element_type=jnp.float32)
    for n, part in enumerate(parts):
        value = jnp.where(where == part, every[n * rows : (n + 1) * rows, :], value)
    return value


def pick_ceiling(halves, rows, widths, where, onehot, states, got):
    size = onehot.shape[0]
    mine = lax.axis_index("st")
    per = size // LANES
    tops, parts = [], []
    for h in range(halves):
        c = got[h][rows * widths[0] // LANES :, :].astype(jnp.float32)
        for k in range(states // size):
            tops.append(rows_to_lanes(c, k * per, per))
            parts.append(((mine + h) % halves) * (states // size) + k)
    every = jnp.dot(
        jnp.concatenate(tops, axis=0).astype(jnp.bfloat16), onehot, preferred_element_type=jnp.float32
    )
    ceiling = jnp.zeros(where.shape, jnp.float32)
    for n, part in enumerate(parts):
        ceiling = jnp.where(where == part, every[n : n + 1, :], ceiling)
    return ceiling


def pick_kernel(halves, widths, chunks, where_ref, onehot_ref, *refs):
    value_ref, ceiling_ref = refs[-2:]
    got = [refs[n * halves : (n + 1) * halves] for n in range(len(chunks))]
    rest = refs[halves * len(chunks) : -2]
    where, onehot, states = where_ref[...], onehot_ref[...], where_ref.shape[1]
    value = rest[0][...] if rest else jnp.zeros(value_ref.shape, jnp.float32)
    for chunk, per_core in zip(chunks, got):
        value = pick(halves, range(halves), widths, chunk, where, onehot, states, per_core, value)
    value_ref[...] = value
    if chunks[0] == 0:
        ceiling_ref[...] = pick_ceiling(halves, value.shape[0], widths, where, onehot, states, got[0])
    else:
        ceiling_ref[...] = rest[1][...]


def picked(halves, rows, widths, chunks, marks, got, before=()):
    where, onehot = marks
    states = where.shape[1]
    outs = [((rows, states), jnp.float32), ((1, states), jnp.float32)]
    args = [where, onehot, *[x for per_core in got for x in per_core], *before]
    kernel = functools.partial(pick_kernel, halves, widths, chunks)
    width = sum(widths[c] for c in chunks)
    return call(kernel, outs, 2 * rows * states * width * halves, 4 * rows * states, args)


def settle_kernel(halves, widths, turns, utility_ref, where_ref, onehot_ref, own_ref, top_ref, *refs):
    known_ref, base_ref = refs[3 * turns : 3 * turns + 2]
    scale_refs = refs[3 * turns + 2 :]
    where, onehot, states = where_ref[...], onehot_ref[...], where_ref.shape[1]
    tops = [top_ref[...]] + [refs[3 * n + 2][...] for n in range(turns)]
    ceiling = functools.reduce(jnp.maximum, tops)
    known = own_ref[...] * jnp.exp(tops[0] - ceiling)
    for n in range(turns):
        scale = jnp.exp(tops[n + 1] - ceiling)
        value = pick(halves, (0,), widths, len(widths) - 1, where, onehot, states, refs[3 * n : 3 * n + 1], refs[3 * n + 1][...])
        known += scale * value
        scale_refs[n][...] = scale
    known_ref[...] = known
    base_ref[...] = utility_ref[...] + DISCOUNT * ceiling


def settle(halves, widths, utility, marks, own, others):
    rows, states = utility.shape
    args = [utility, *marks, *own]
    for got, before in others:
        args += [got, *before]
    outs = [((rows, states), jnp.float32)] * 2 + [((1, states), jnp.float32)] * len(others)
    kernel = functools.partial(settle_kernel, halves, widths, len(others))
    flops = 2 * rows * states * widths[-1] * len(others)
    return call(kernel, outs, flops, 16 * rows * states, args)


def finish_kernel(halves, widths, turns, tile, where_ref, onehot_ref, known_ref, base_ref, *refs):
    *refs, out_ref, held_ref, sems = refs
    rows, states = known_ref.shape
    copies = []
    for start in range(0, states, tile):
        here = slice(start, start + tile)
        where, onehot = where_ref[:, here], onehot_ref[:, here]
        merged = known_ref[:, here]
        for n in range(turns):
            got = refs[turns + n * (halves - 1) : turns + (n + 1) * (halves - 1)]
            zero = jnp.zeros((rows, tile), jnp.float32)
            value = pick(halves, range(1, halves), widths, len(widths) - 1, where, onehot, states, got, zero)
            merged += refs[n][:, here] * value
        held_ref[:, here] = base_ref[:, here] + DISCOUNT * jnp.log(merged)
        copy = pltpu.make_async_copy(held_ref.at[:, here], out_ref.at[:, here], sems.at[start // tile])
        copy.start()
        copies.append(copy)
    for copy in copies:
        copy.wait()


def finish(halves, widths, marks, settled, others):
    known, base, *scales = settled
    rows, states = known.shape
    args = [*marks, known, base, *scales, *[x for got in others for x in got]]
    kernel = functools.partial(finish_kernel, halves, widths, len(others), states // TILES)
    flops = 2 * rows * states * widths[-1] * (halves - 1) * len(others)
    return pl.pallas_call(
        kernel,
        in_specs=[pl.BlockSpec(memory_space=pltpu.VMEM)] * len(args),
        out_specs=pl.BlockSpec(memory_space=pltpu.HBM),
        out_shape=pltpu.HBM((rows, states), jnp.float32),
        scratch_shapes=[pltpu.VMEM((rows, states), jnp.float32), pltpu.SemaphoreType.DMA((TILES,))],
        compiler_params=pltpu.CompilerParams(vmem_limit_bytes=GRANT),
        cost_estimate=pl.CostEstimate(flops=flops, bytes_accessed=12 * rows * states, transcendentals=0),
        name="finish",
    )(*[pltpu.with_memory_space_constraint(a, pltpu.VMEM) for a in args])


def on_device(sizes, value_now, utility, move_costs, dest_blocks, row_counts, transition):
    dest, orig, halves = sizes
    low = 2 if dest % 2 == 0 else 1
    high = dest // low
    rows, states = value_now.shape[2:]
    pieces = states // 2**LOW_BITS
    widths = tuple((pieces + CHUNKS - 1 - c) // CHUNKS * 2**LOW_BITS for c in range(CHUNKS))
    every = tuple(range(CHUNKS))
    both = ("dst", "org")

    def index(h, l, o):
        return (h * low + l) * orig + o

    def gather(x, i, j):
        pairs = [
            (index(h, l, o), index(h, (l - i) % low, (o - j) % orig))
            for h in range(high)
            for l in range(low)
            for o in range(orig)
        ]
        return lax.ppermute(x, both, pairs)

    def onward(x, r):
        pairs = [(h * low + l, ((h + r) % high) * low + l) for h in range(high) for l in range(low)]
        return lax.ppermute(x, "dst", pairs)

    def across(x):
        pairs = [[(s, (s - h) % halves) for s in range(halves)] for h in range(halves)]
        return [x if h == 0 else lax.ppermute(x, "st", pairs[h]) for h in range(halves)]

    cost = move_costs.reshape(move_costs.shape[0], rows, move_costs.shape[4])
    made = weigh(high, low, orig, widths, value_now.reshape(rows, states), cost)
    plain, keyed, own_key = made[:CHUNKS], made[CHUNKS:-1], made[-1]
    gathered = []
    for c in every:
        row = []
        for i in range(low):
            for j in range(orig):
                x = keyed[i - 1] if c == 0 and i > 0 and j == 0 else plain[c]
                row.append(x if i == j == 0 else gather(x, i, j))
        gathered.append(row)
    *marks, open_to = spot(high, low, orig, halves, transition, row_counts, dest_blocks)
    step = functools.partial(sums, low, orig, rows)
    rest = (open_to, own_key, gathered)
    turns = tuple(range(1, high))
    passed = []
    for c in every:
        sent = step(c, widths, turns, *rest) if turns else []
        passed.append([onward(x, r) for r, x in zip(turns, sent)])
    own = []
    for c in every:
        own += step(c, widths, (0,), *rest)
    own = [across(x) for x in own]
    own = picked(halves, rows, widths, every, marks, own)
    near, far = [], []
    for n in range(len(turns)):
        before = ()
        for c in every[:-1]:
            got = across(passed[c][n])
            before = picked(halves, rows, widths, (c,), marks, [got], before)
        here, *there = across(passed[-1][n])
        near.append((here, before))
        far.append(there)
    settled = settle(halves, widths, utility.reshape(rows, states), marks, own, near)
    out = finish(halves, widths, marks, settled, far)
    return out.reshape(value_now.shape)


def solution(mesh):
    sizes = (mesh.shape["dst"], mesh.shape["org"], mesh.shape["st"])

    def body(*args):
        return on_device(sizes, *args)

    return jax.shard_map(
        body,
        mesh=mesh,
        in_specs=(
            P(("draws", "dst"), "org", None, "st"),
            P(("draws", "dst"), "org", None, "st"),
            P("draws", "org", None, "dst", None),
            P(),
            P(),
            P(),
        ),
        out_specs=P(("draws", "dst"), "org", None, "st"),
        check_vma=False,
    )
```

profile of v0, /device:TPU:0, one launch (start us, length us, event | category | flops | bytes accessed | tf_op | source)
XLA Modules:
  0.0 33.3 jit_solution(3561670255879984017)
XLA Ops:
  0.0 0.0 copy-start.2
  0.0 1.3 %shard_map.65 = (bf16[528,128]{1,0:T(8,128)(2,1)S(1)}, bf16[512,128]{1,0:T(8,128)(2,1)S(1)}, bf16[656,128]{1,0:T(8,128)(2,1)S(1)}, bf16[128,128]{1,0:T(8,128)(2,1)S(1)}) custom-call(f32[64,2048]{1,0:T(8,128)} %bitcast.5, f32[4,64,128]{2,1,0:T(8,128)} %bitcast.6), custom_call_target="tpu_custom_call" | custom-call | flops 1048576 | bytes 1048576 | tf_op jit(solution)/shard_map/pallas_call | solution.py:27
  1.3 3.0 %collective-permute-start = (bf16[528,128]{1,0:T(8,128)(2,1)S(1)}, bf16[528,128]{1,0:T(8,128)(2,1)S(1)}, u32[]{:S(2)}, u32[]{:S(2)}) collective-permute-start(bf16[528,128]{1,0:T(8,128)(2,1)S(1)} %get-tuple-element.23.refs_0_), channel_id=1, source_target_pairs={{0,2},{2,0},{4,6},{6,4},{8,10},{10,8},{12,14},{14,12},{1,3},{3,1},... | collective-permute-start | bytes 405512 | tf_op jit(solution)/shard_map/ppermute | solution.py:346
  4.3 1.6 %collective-permute-start.1 = (bf16[656,128]{1,0:T(8,128)(2,1)S(1)}, bf16[656,128]{1,0:T(8,128)(2,1)S(1)}, u32[]{:S(2)}, u32[]{:S(2)}) collective-permute-start(bf16[656,128]{1,0:T(8,128)(2,1)S(1)} %get-tuple-element.24), channel_id=1, source_target_pairs={{0,4},{2,6},{4,0},{6,2},{8,12},{10,14},{12,8},{14,10},{1,5},{3,7},... | collective-permute-start | bytes 503816 | tf_op jit(solution)/shard_map/ppermute | solution.py:346
  5.9 0.0 collective-permute-start.2
  5.9 0.0 copy-start.3
  5.9 1.9 %collective-permute-start.4 = (bf16[512,128]{1,0:T(8,128)(2,1)S(1)}, bf16[512,128]{1,0:T(8,128)(2,1)S(1)}, u32[]{:S(2)}, u32[]{:S(2)}) collective-permute-start(bf16[512,128]{1,0:T(8,128)(2,1)S(1)} %get-tuple-element.25.refs_4_), channel_id=1, source_target_pairs={{0,2},{2,0},{4,6},{6,4},{8,10},{10,8},{12,14},{14,12},{1,3},{3,1},... | collective-permute-start | bytes 393224 | tf_op jit(solution)/shard_map/ppermute | solution.py:346
  7.8 1.6 %collective-permute-start.5 = (bf16[512,128]{1,0:T(8,128)(2,1)S(1)}, bf16[512,128]{1,0:T(8,128)(2,1)S(1)}, u32[]{:S(2)}, u32[]{:S(2)}) collective-permute-start(bf16[512,128]{1,0:T(8,128)(2,1)S(1)} %get-tuple-element.25.refs_4_), channel_id=1, source_target_pairs={{0,4},{2,6},{4,0},{6,2},{8,12},{10,14},{12,8},{14,10},{1,5},{3,7},... | collective-permute-start | bytes 393224 | tf_op jit(solution)/shard_map/ppermute | solution.py:346
  9.4 0.0 collective-permute-done.refs_1_
  9.4 1.5 %collective-permute-start.6 = (bf16[512,128]{1,0:T(8,128)(2,1)S(1)}, bf16[512,128]{1,0:T(8,128)(2,1)S(1)}, u32[]{:S(2)}, u32[]{:S(2)}) collective-permute-start(bf16[512,128]{1,0:T(8,128)(2,1)S(1)} %get-tuple-element.25.refs_4_), channel_id=1, source_target_pairs={{0,6},{2,4},{4,2},{6,0},{8,14},{10,12},{12,10},{14,8},{1,7},{3,5},... | collective-permute-start | bytes 393224 | tf_op jit(solution)/shard_map/ppermute | solution.py:346
  10.9 0.0 copy-done.2
  10.9 0.0 copy-done.3
  10.9 0.0 copy-start.1
  10.9 0.1 copy.7.list_ref
  11.0 0.6 %copy-done.1 = s32[8]{0:T(128)S(1)} copy-done((s32[8]{0:T(128)S(1)}, s32[8]{0:T(128)}, u32[]{:S(2)}) %copy-start.1) | copy-done | bytes 56
  11.6 0.8 %shard_map.64 = (s32[1,2048]{1,0:T(1,128)S(1)}, bf16[256,2048]{1,0:T(8,128)(2,1)S(1)}, f32[8,128]{1,0:T(8,128)S(1)}) custom-call(s32[2,2048]{1,0:T(2,128)S(1)} %reshape.15.transition_ref, s32[8]{0:T(128)S(1)} %copy-done.1, s32[8,3]{1,0:T(8,128)S(1)} %copy.7.list_ref), custom_call_target="tpu_custom_call" | custom-call | flops 2097152 | bytes 1048576 | tf_op jit(solution)/shard_map/pallas_call | solution.py:27
  12.4 1.5 %collective-permute-done.2.refs_3_ = bf16[528,128]{1,0:T(8,128)(2,1)S(1)} collective-permute-done((bf16[528,128]{1,0:T(8,128)(2,1)S(1)}, bf16[528,128]{1,0:T(8,128)(2,1)S(1)}, u32[]{:S(2)}, u32[]{:S(2)}) %collective-permute-start.2) | collective-permute-done | bytes 135200 | tf_op jit(solution)/shard_map/ppermute | solution.py:346
  13.9 0.0 collective-permute-done.1.refs_2_
  13.9 0.3 shard_map.70
  14.2 3.1 %collective-permute-start.9 = (bf16[528,128]{1,0:T(8,128)(2,1)S(1)}, bf16[528,128]{1,0:T(8,128)(2,1)S(1)}, u32[]{:S(2)}, u32[]{:S(2)}) collective-permute-start(bf16[528,128]{1,0:T(8,128)(2,1)S(1)} %shard_map.70), channel_id=1, source_target_pairs={{0,8},{4,12},{8,0},{12,4},{1,9},{5,13},{9,1},{13,5},{2,10},{6,14},... | collective-permute-start | bytes 405512 | tf_op jit(solution)/shard_map/ppermute | solution.py:350
  17.3 0.3 shard_map.66.refs_0_
  17.6 0.1 collective-permute-start.3
  17.7 0.0 collective-permute-done.4.refs_5_
  17.7 1.0 %collective-permute-done.5.refs_6_ = bf16[512,128]{1,0:T(8,128)(2,1)S(1)} collective-permute-done((bf16[512,128]{1,0:T(8,128)(2,1)S(1)}, bf16[512,128]{1,0:T(8,128)(2,1)S(1)}, u32[]{:S(2)}, u32[]{:S(2)}) %collective-permute-start.5) | collective-permute-done | bytes 131104 | tf_op jit(solution)/shard_map/ppermute | solution.py:346
  18.6 1.2 %collective-permute-done.6.refs_7_ = bf16[512,128]{1,0:T(8,128)(2,1)S(1)} collective-permute-done((bf16[512,128]{1,0:T(8,128)(2,1)S(1)}, bf16[512,128]{1,0:T(8,128)(2,1)S(1)}, u32[]{:S(2)}, u32[]{:S(2)}) %collective-permute-start.6) | collective-permute-done | bytes 131104 | tf_op jit(solution)/shard_map/ppermute | solution.py:346
  19.8 0.3 shard_map.69
  20.1 2.7 %collective-permute-start.8 = (bf16[512,128]{1,0:T(8,128)(2,1)S(1)}, bf16[512,128]{1,0:T(8,128)(2,1)S(1)}, u32[]{:S(2)}, u32[]{:S(2)}) collective-permute-start(bf16[512,128]{1,0:T(8,128)(2,1)S(1)} %shard_map.69), channel_id=1, source_target_pairs={{0,8},{4,12},{8,0},{12,4},{1,9},{5,13},{9,1},{13,5},{2,10},{6,14},... | collective-permute-start | bytes 393224 | tf_op jit(solution)/shard_map/ppermute | solution.py:350
  22.9 0.3 shard_map.67.refs_2_
  23.2 0.1 collective-permute-start.7
  23.3 0.0 collective-permute-done.9.refs_0_
  23.3 0.5 %collective-permute-start.10 = (bf16[528,128]{1,0:T(8,128)(2,1)S(1)}, bf16[528,128]{1,0:T(8,128)(2,1)S(1)}, u32[]{:S(2)}, u32[]{:S(2)}) collective-permute-start(bf16[528,128]{1,0:T(8,128)(2,1)S(1)} %collective-permute-done.9.refs_0_), channel_id=1, source_target_pairs={{0,1},{1,0},{2,3},{3,2},{4,5},{5,4},{6,7},{7,6},{8,9},{9,8},{10,11... | collective-permute-start | bytes 405512 | tf_op jit(solution)/shard_map/ppermute | solution.py:354
  23.8 5.4 %collective-permute-done.8.refs_0_ = bf16[512,128]{1,0:T(8,128)(2,1)S(1)} collective-permute-done((bf16[512,128]{1,0:T(8,128)(2,1)S(1)}, bf16[512,128]{1,0:T(8,128)(2,1)S(1)}, u32[]{:S(2)}, u32[]{:S(2)}) %collective-permute-start.8) | collective-permute-done | bytes 131104 | tf_op jit(solution)/shard_map/ppermute | solution.py:350
  29.1 0.0 collective-permute-start.11
  29.1 0.0 collective-permute-done.7.refs_3_
  29.1 0.0 collective-permute-done.3.refs_1_
  29.1 1.4 %shard_map.68 = (f32[64,2048]{1,0:T(8,128)S(1)}, f32[1,2048]{1,0:T(1,128)S(1)}) custom-call(s32[1,2048]{1,0:T(1,128)S(1)} %get-tuple-element.19.where_ref, bf16[256,2048]{1,0:T(8,128)(2,1)S(1)} %get-tuple-element.20.onehot_ref, bf16[528,128]{1,0:T(8,128)(2,1)S(1)} %shard_map.66.refs_0_, bf16[528,128]{1,0:T(8,128)(2,1)S(1)} %collective-permute-done.3.refs_1_, ...), custom_call_target="tpu_custom_call" | custom-call | flops 1073741824 | bytes 524288 | tf_op jit(solution)/shard_map/pallas_call | solution.py:27
  30.6 0.0 copy-start
  30.6 0.0 collective-permute-done.10.refs_1_
  30.6 0.8 %shard_map.71 = (f32[64,2048]{1,0:T(8,128)S(1)}, f32[1,2048]{1,0:T(1,128)S(1)}) custom-call(s32[1,2048]{1,0:T(1,128)S(1)} %get-tuple-element.19.where_ref, bf16[256,2048]{1,0:T(8,128)(2,1)S(1)} %get-tuple-element.20.onehot_ref, bf16[528,128]{1,0:T(8,128)(2,1)S(1)} %collective-permute-done.9.refs_0_, bf16[528,128]{1,0:T(8,128)(2,1)S(1)} %collective-permute-done.10.refs_1_), custom_call_target="tpu_custom_call" | custom-call | flops 536870912 | bytes 524288 | tf_op jit(solution)/shard_map/pallas_call | solution.py:27
  31.4 0.2 copy-done
  31.6 0.5 %shard_map.72 = (f32[64,2048]{1,0:T(8,128)S(1)}, f32[64,2048]{1,0:T(8,128)S(1)}, f32[1,2048]{1,0:T(1,128)S(1)}) custom-call(f32[64,2048]{1,0:T(8,128)S(1)} %bitcast.4, s32[1,2048]{1,0:T(1,128)S(1)} %get-tuple-element.19.where_ref, bf16[256,2048]{1,0:T(8,128)(2,1)S(1)} %get-tuple-element.20.onehot_ref, f32[64,2048]{1,0:T(8,128)S(1)} %get-tuple-element.26.own_ref, ...), custom_call_target="tpu_custom_call" | custom-call | flops 268435456 | bytes 2097152 | tf_op jit(solution)/shard_map/pallas_call | solution.py:27
  32.1 0.0 collective-permute-done.11.refs_1_
  32.1 1.2 %finish.1 = f32[64,2048]{1,0:T(8,128)} custom-call(s32[1,2048]{1,0:T(1,128)S(1)} %get-tuple-element.19.where_ref, bf16[256,2048]{1,0:T(8,128)(2,1)S(1)} %get-tuple-element.20.onehot_ref, f32[64,2048]{1,0:T(8,128)S(1)} %get-tuple-element.30.known_ref, f32[64,2048]{1,0:T(8,128)S(1)} %get-tuple-element.31.base_ref, f32[1,2048]{1,0:T(1,128)S(1)} %get-tuple-element.32.refs_0_, ...), custom_call_target="tpu_custom_call" | custom-call | flops 268435456 | bytes 1572864 | tf_op jit(solution)/shard_map/finish/pallas_call | solution.py:314
  (1 shorter events, 0.0 us)
Async XLA Ops:
  0.0 10.9 %copy-start.2 = (s32[4096]{0:T(1024)S(1)}, s32[4096]{0:T(1024)}, u32[]{:S(2)}) copy-start(s32[4096]{0:T(1024)} %param.11) | copy-start | bytes 49156
  1.3 8.1 %collective-permute-start = (bf16[528,128]{1,0:T(8,128)(2,1)S(1)}, bf16[528,128]{1,0:T(8,128)(2,1)S(1)}, u32[]{:S(2)}, u32[]{:S(2)}) collective-permute-start(bf16[528,128]{1,0:T(8,128)(2,1)S(1)} %get-tuple-element.23.refs_0_), channel_id=1, source_target_pairs={{0,2},{2,0},{4,6},{6,4},{8,10},{10,8},{12,14},{14,12},{1,3},{3,1},... | collective-permute-start | bytes 405512 | tf_op jit(solution)/shard_map/ppermute | solution.py:346
  4.3 9.6 %collective-permute-start.1 = (bf16[656,128]{1,0:T(8,128)(2,1)S(1)}, bf16[656,128]{1,0:T(8,128)(2,1)S(1)}, u32[]{:S(2)}, u32[]{:S(2)}) collective-permute-start(bf16[656,128]{1,0:T(8,128)(2,1)S(1)} %get-tuple-element.24), channel_id=1, source_target_pairs={{0,4},{2,6},{4,0},{6,2},{8,12},{10,14},{12,8},{14,10},{1,5},{3,7},... | collective-permute-start | bytes 503816 | tf_op jit(solution)/shard_map/ppermute | solution.py:346
  5.9 8.0 %collective-permute-start.2 = (bf16[528,128]{1,0:T(8,128)(2,1)S(1)}, bf16[528,128]{1,0:T(8,128)(2,1)S(1)}, u32[]{:S(2)}, u32[]{:S(2)}) collective-permute-start(bf16[528,128]{1,0:T(8,128)(2,1)S(1)} %get-tuple-element.23.refs_0_), channel_id=1, source_target_pairs={{0,6},{2,4},{4,2},{6,0},{8,14},{10,12},{12,10},{14,8},{1,7},{3,5},... | collective-permute-start | bytes 405512 | tf_op jit(solution)/shard_map/ppermute | solution.py:346
  5.9 5.0 %copy-start.3 = (s32[8,3]{0,1:T(4,128)S(1)}, s32[8,3]{0,1:T(4,128)}, u32[]{:S(2)}) copy-start(s32[8,3]{0,1:T(4,128)} %param.9) | copy-start | bytes 292
  5.9 11.8 %collective-permute-start.4 = (bf16[512,128]{1,0:T(8,128)(2,1)S(1)}, bf16[512,128]{1,0:T(8,128)(2,1)S(1)}, u32[]{:S(2)}, u32[]{:S(2)}) collective-permute-start(bf16[512,128]{1,0:T(8,128)(2,1)S(1)} %get-tuple-element.25.refs_4_), channel_id=1, source_target_pairs={{0,2},{2,0},{4,6},{6,4},{8,10},{10,8},{12,14},{14,12},{1,3},{3,1},... | collective-permute-start | bytes 393224 | tf_op jit(solution)/shard_map/ppermute | solution.py:346
  7.8 10.8 %collective-permute-start.5 = (bf16[512,128]{1,0:T(8,128)(2,1)S(1)}, bf16[512,128]{1,0:T(8,128)(2,1)S(1)}, u32[]{:S(2)}, u32[]{:S(2)}) collective-permute-start(bf16[512,128]{1,0:T(8,128)(2,1)S(1)} %get-tuple-element.25.refs_4_), channel_id=1, source_target_pairs={{0,4},{2,6},{4,0},{6,2},{8,12},{10,14},{12,8},{14,10},{1,5},{3,7},... | collective-permute-start | bytes 393224 | tf_op jit(solution)/shard_map/ppermute | solution.py:346
  9.4 10.4 %collective-permute-start.6 = (bf16[512,128]{1,0:T(8,128)(2,1)S(1)}, bf16[512,128]{1,0:T(8,128)(2,1)S(1)}, u32[]{:S(2)}, u32[]{:S(2)}) collective-permute-start(bf16[512,128]{1,0:T(8,128)(2,1)S(1)} %get-tuple-element.25.refs_4_), channel_id=1, source_target_pairs={{0,6},{2,4},{4,2},{6,0},{8,14},{10,12},{12,10},{14,8},{1,7},{3,5},... | collective-permute-start | bytes 393224 | tf_op jit(solution)/shard_map/ppermute | solution.py:346
  10.9 0.7 %copy-start.1 = (s32[8]{0:T(128)S(1)}, s32[8]{0:T(128)}, u32[]{:S(2)}) copy-start(s32[8]{0:T(128)} %count_ref.1) | copy-start | bytes 100
  14.2 9.1 %collective-permute-start.9 = (bf16[528,128]{1,0:T(8,128)(2,1)S(1)}, bf16[528,128]{1,0:T(8,128)(2,1)S(1)}, u32[]{:S(2)}, u32[]{:S(2)}) collective-permute-start(bf16[528,128]{1,0:T(8,128)(2,1)S(1)} %shard_map.70), channel_id=1, source_target_pairs={{0,8},{4,12},{8,0},{12,4},{1,9},{5,13},{9,1},{13,5},{2,10},{6,14},... | collective-permute-start | bytes 405512 | tf_op jit(solution)/shard_map/ppermute | solution.py:350
  17.6 11.6 %collective-permute-start.3 = (bf16[528,128]{1,0:T(8,128)(2,1)S(1)}, bf16[528,128]{1,0:T(8,128)(2,1)S(1)}, u32[]{:S(2)}, u32[]{:S(2)}) collective-permute-start(bf16[528,128]{1,0:T(8,128)(2,1)S(1)} %shard_map.66.refs_0_), channel_id=1, source_target_pairs={{0,1},{1,0},{2,3},{3,2},{4,5},{5,4},{6,7},{7,6},{8,9},{9,8},{10,11... | collective-permute-start | bytes 405512 | tf_op jit(solution)/shard_map/ppermute | solution.py:354
  20.1 9.0 %collective-permute-start.8 = (bf16[512,128]{1,0:T(8,128)(2,1)S(1)}, bf16[512,128]{1,0:T(8,128)(2,1)S(1)}, u32[]{:S(2)}, u32[]{:S(2)}) collective-permute-start(bf16[512,128]{1,0:T(8,128)(2,1)S(1)} %shard_map.69), channel_id=1, source_target_pairs={{0,8},{4,12},{8,0},{12,4},{1,9},{5,13},{9,1},{13,5},{2,10},{6,14},... | collective-permute-start | bytes 393224 | tf_op jit(solution)/shard_map/ppermute | solution.py:350
  23.2 6.0 %collective-permute-start.7 = (bf16[512,128]{1,0:T(8,128)(2,1)S(1)}, bf16[512,128]{1,0:T(8,128)(2,1)S(1)}, u32[]{:S(2)}, u32[]{:S(2)}) collective-permute-start(bf16[512,128]{1,0:T(8,128)(2,1)S(1)} %shard_map.67.refs_2_), channel_id=1, source_target_pairs={{0,1},{1,0},{2,3},{3,2},{4,5},{5,4},{6,7},{7,6},{8,9},{9,8},{10,11... | collective-permute-start | bytes 393224 | tf_op jit(solution)/shard_map/ppermute | solution.py:354
  23.3 7.3 %collective-permute-start.10 = (bf16[528,128]{1,0:T(8,128)(2,1)S(1)}, bf16[528,128]{1,0:T(8,128)(2,1)S(1)}, u32[]{:S(2)}, u32[]{:S(2)}) collective-permute-start(bf16[528,128]{1,0:T(8,128)(2,1)S(1)} %collective-permute-done.9.refs_0_), channel_id=1, source_target_pairs={{0,1},{1,0},{2,3},{3,2},{4,5},{5,4},{6,7},{7,6},{8,9},{9,8},{10,11... | collective-permute-start | bytes 405512 | tf_op jit(solution)/shard_map/ppermute | solution.py:354
  29.1 3.0 %collective-permute-start.11 = (bf16[512,128]{1,0:T(8,128)(2,1)S(1)}, bf16[512,128]{1,0:T(8,128)(2,1)S(1)}, u32[]{:S(2)}, u32[]{:S(2)}) collective-permute-start(bf16[512,128]{1,0:T(8,128)(2,1)S(1)} %collective-permute-done.8.refs_0_), channel_id=1, source_target_pairs={{0,1},{1,0},{2,3},{3,2},{4,5},{5,4},{6,7},{7,6},{8,9},{9,8},{10,11... | collective-permute-start | bytes 393224 | tf_op jit(solution)/shard_map/ppermute | solution.py:354
  30.6 1.0 %copy-start = (f32[1,1,64,2048]{3,2,1,0:T(8,128)S(1)}, f32[1,1,64,2048]{3,2,1,0:T(8,128)}, u32[]{:S(2)}) copy-start(f32[1,1,64,2048]{3,2,1,0:T(8,128)} %param.7) | copy-start | bytes 1572868
where the time goes:
time: 33.5 us; the launch traced here: 33.3 us
  starting transfers between devices  16.1 us (48%)
  waiting for transfers between devices  9.06 us (27%)
  Pallas kernels  7.17 us (21%)
  local copies, waits for them, and re-layouts  0.84 us (3%)
    ppermute x6, starting transfers between devices, gather(): return lax.ppermute(x, both, pairs)  9.6 us
    pallas_call x9, Pallas kernels, call(): pl.pallas_call(kernel, in_specs=specs, out_specs=[pl.BlockSpec(memory_spa...  5.99 us
    ppermute x2, starting transfers between devices, onward(): return lax.ppermute(x, 'dst', pairs)  5.81 us
    ppermute x2, waiting for transfers between devices, onward(): return lax.ppermute(x, 'dst', pairs)  5.36 us
    ppermute x6, waiting for transfers between devices, gather(): return lax.ppermute(x, both, pairs)  3.69 us
    pallas_call x1, Pallas kernels, finish(): pl.pallas_call(kernel, in_specs=[pl.BlockSpec(memory_space=pltpu.VMEM)] *...  1.18 us
    unnamed x9, local copies, waits for them, and re-layouts  0.83 us
  transfers between devices with their start and end apart: 12, of which 4 were waited for; matrix products, arithmetic and copies ran while one was open for 0% of the time, Pallas kernels for 14%

commit v1 on v0

--- a/solution.py
+++ b/solution.py
@@ -60,7 +60,9 @@
 
 
 def weigh_kernel(high, low, orig, widths, value_ref, cost_ref, *out_refs):
-    plain_refs, keyed_refs, own_ref = out_refs[: len(widths)], out_refs[len(widths) : -1], out_refs[-1]
+    plain_refs, own_ref = out_refs[: len(widths)], out_refs[-1]
+    keyed_refs, late_refs = out_refs[len(widths) : len(widths) + low - 1], out_refs[len(widths) + low - 1 : -1]
+    base = own_ref.shape[0] // high * (high - 1)
     my_high, my_low = place(low)
     my_orig = lax.axis_index("org")
     rows = value_ref.shape[0]
@@ -82,7 +84,9 @@
         at = put(own_ref, at, part)
     for turn in range(1, low):
         at = 0
-        for part in kernel_part(turn):
+        late, *parts = kernel_part(turn)
+        put(late_refs[turn - 1], 0, late)
+        for part in parts:
             at = put(keyed_refs[turn - 1], at, part)
     start = 0
     tops = []
@@ -95,12 +99,12 @@
         if c == 0:
             first = end
             for ref in keyed_refs:
-                put(ref, own_ref.shape[0], e)
+                put(ref, base, e)
         start += width
     packed = lanes_to_rows(jnp.concatenate(tops, axis=1)).astype(jnp.bfloat16)
     plain_refs[0][first:, :] = packed
     for ref in keyed_refs:
-        ref[own_ref.shape[0] + first :, :] = packed
+        ref[base + first :, :] = packed
 
 
 def weigh(high, low, orig, widths, value, cost):
@@ -108,17 +112,19 @@
     tops = states // LANES
     keys = high * rows * cost.shape[2] // LANES
     sizes = [rows * w // LANES + (tops if c == 0 else 0) for c, w in enumerate(widths)]
-    sizes += [keys + sizes[0]] * (low - 1) + [keys]
+    sizes += [keys // high * (high - 1) + sizes[0]] * (low - 1) + [keys // high] * (low - 1) + [keys]
     outs = [((size, LANES), jnp.bfloat16) for size in sizes]
     kernel = functools.partial(weigh_kernel, high, low, orig, widths)
     return call(kernel, outs, 8 * rows * states, 8 * rows * states, (value, cost), fetched=(0, 1))
 
 
-def sums_kernel(low, orig, rows, chunk, widths, turns, open_ref, own_ref, *refs):
+def sums_kernel(high, low, orig, rows, chunk, widths, turns, open_ref, own_ref, *refs):
     groups = low * orig
     width = widths[chunk]
     first = sum(widths[:chunk]) // LANES
-    keys = own_ref.shape[0]
+    keys = own_ref.shape[0] // high * (high - 1)
+    late = low - 1 if 0 in turns else 0
+    late_refs, refs = refs[:late], refs[late:]
     skips = [keys if b >= orig and b % orig == 0 else 0 for b in range(groups)]
     ends = [skip + rows * widths[0] // LANES for skip in skips]
     tops = [refs[b][ends[b] :, :].astype(jnp.float32) for b in range(groups)]
@@ -129,11 +135,13 @@
         ceiling = functools.reduce(jnp.maximum, [jnp.where(f, t, FLOOR) for f, t in zip(feasible, tops)])
         total = jnp.zeros((rows, width), jnp.float32)
         for i in range(low):
-            key_ref = own_ref if i == 0 else refs[i * orig]
+            key_ref, nth = own_ref, turn
+            if i > 0:
+                key_ref, nth = (late_refs[i - 1], 0) if turn == 0 else (refs[i * orig], turn - 1)
             for j in range(orig):
                 b = i * orig + j
                 scale = jnp.exp(jnp.where(feasible[b], tops[b] - ceiling, FLOOR))
-                column = (turn * orig + j) * rows
+                column = (nth * orig + j) * rows
                 at, column = column // LANES * rows, column % LANES
                 product = jnp.dot(
                     key_ref[at : at + rows, column : column + rows],
@@ -146,15 +154,15 @@
             out_refs[n][end:, :] = ceiling.astype(jnp.bfloat16)
 
 
-def sums(low, orig, rows, chunk, widths, turns, open_to, own_key, gathered):
+def sums(high, low, orig, rows, chunk, widths, turns, open_to, own_key, late, gathered):
     width = widths[chunk]
     groups = low * orig
-    args = [open_to, own_key, *gathered[0]]
+    args = [open_to, own_key, *(late if 0 in turns else ()), *gathered[0]]
     if chunk > 0:
         args += gathered[chunk]
     size = rows * width // LANES + (sum(widths) // LANES if chunk == 0 else 0)
     outs = [((size, LANES), jnp.bfloat16)] * len(turns)
-    kernel = functools.partial(sums_kernel, low, orig, rows, chunk, widths, turns)
+    kernel = functools.partial(sums_kernel, high, low, orig, rows, chunk, widths, turns)
     flops = 2 * rows * rows * width * groups * len(turns)
     return call(kernel, outs, flops, 2 * rows * width * (groups + len(turns)), args)
 
@@ -355,7 +363,9 @@
 
     cost = move_costs.reshape(move_costs.shape[0], rows, move_costs.shape[4])
     made = weigh(high, low, orig, widths, value_now.reshape(rows, states), cost)
-    plain, keyed, own_key = made[:CHUNKS], made[CHUNKS:-1], made[-1]
+    plain, own_key = made[:CHUNKS], made[-1]
+    keyed, late = made[CHUNKS : CHUNKS + low - 1], made[CHUNKS + low - 1 : -1]
+    late = [gather(x, i, 0) for i, x in enumerate(late, 1)]
     gathered = []
     for c in every:
         row = []
@@ -365,8 +375,8 @@
                 row.append(x if i == j == 0 else gather(x, i, j))
         gathered.append(row)
     *marks, open_to = spot(high, low, orig, halves, transition, row_counts, dest_blocks)
-    step = functools.partial(sums, low, orig, rows)
-    rest = (open_to, own_key, gathered)
+    step = functools.partial(sums, high, low, orig, rows)
+    rest = (open_to, own_key, late, gathered)
     turns = tuple(range(1, high))
     passed = []
     for c in every:

time: 33.5 us -> 36.2 us (1.081)
  starting transfers between devices: 16.1 us -> 17.9 us
  waiting for transfers between devices: 9.06 us -> 9.91 us
    ppermute x6 -> x7, starting transfers between devices: 9.6 us -> 11.7 us  [gather(): return lax.ppermute(x, both, pairs)]
    ppermute x2, waiting for transfers between devices: 5.36 us -> 6.12 us  [onward(): return lax.ppermute(x, 'dst', pairs)]
    ppermute x6 -> x7, waiting for transfers between devices: 3.69 us -> 3.78 us  [gather(): return lax.ppermute(x, both, pairs)]
  transfers between devices with their start and end apart: 12 -> 13, of which waited for: 4 -> 3; matrix products, arithmetic and copies ran while one was open for 0% -> 0% of each run, Pallas kernels for 14% -> 13%
where the time goes in v1:
time: 36.2 us; the launch traced here: 36 us
  starting transfers between devices  17.9 us (49%)
  waiting for transfers between devices  9.91 us (27%)
  Pallas kernels  7.18 us (20%)
  local copies, waits for them, and re-layouts  0.85 us (2%)
    ppermute x7, starting transfers between devices, gather(): return lax.ppermute(x, both, pairs)  11.7 us
    ppermute x2, waiting for transfers between devices, onward(): return lax.ppermute(x, 'dst', pairs)  6.12 us
    pallas_call x9, Pallas kernels, call(): pl.pallas_call(kernel, in_specs=specs, out_specs=[pl.BlockSpec(memory_spa...  6 us
    ppermute x2, starting transfers between devices, onward(): return lax.ppermute(x, 'dst', pairs)  5.59 us
    ppermute x7, waiting for transfers between devices, gather(): return lax.ppermute(x, both, pairs)  3.78 us
    pallas_call x1, Pallas kernels, finish(): pl.pallas_call(kernel, in_specs=[pl.BlockSpec(memory_space=pltpu.VMEM)] *...  1.17 us
    unnamed x9, local copies, waits for them, and re-layouts  0.83 us
  transfers between devices with their start and end apart: 13, of which 3 were waited for; matrix products, arithmetic and copies ran while one was open for 0% of the time, Pallas kernels for 13%

profile of v1, /device:TPU:0, one launch (start us, length us, event | category | flops | bytes accessed | tf_op | source)
XLA Modules:
  0.0 36.0 jit_solution(5343118850836001906)
XLA Ops:
  0.0 0.0 copy-start.2
  0.0 1.3 %shard_map.65 = (bf16[528,128]{1,0:T(8,128)(2,1)S(1)}, bf16[512,128]{1,0:T(8,128)(2,1)S(1)}, bf16[592,128]{1,0:T(8,128)(2,1)S(1)}, bf16[64,128]{1,0:T(8,128)(2,1)S(1)}, bf16[128,128]{1,0:T(8,128)(2,1)S(1)}) custom-call(f32[64,2048]{1,0:T(8,128)} %bitcast.5, f32[4,64,128]{2,1,0:T(8,128)} %bitcast.6), custom_call_target="tpu_custom_call" | custom-call | flops 1048576 | bytes 1048576 | tf_op jit(solution)/shard_map/pallas_call | solution.py:27
  1.3 3.0 %collective-permute-start.1 = (bf16[528,128]{1,0:T(8,128)(2,1)S(1)}, bf16[528,128]{1,0:T(8,128)(2,1)S(1)}, u32[]{:S(2)}, u32[]{:S(2)}) collective-permute-start(bf16[528,128]{1,0:T(8,128)(2,1)S(1)} %get-tuple-element.25.refs_1_.refs_0_), channel_id=1, source_target_pairs={{0,2},{2,0},{4,6},{6,4},{8,10},{10,8},{12,14},{14,12},{1,3},{3,1},... | collective-permute-start | bytes 405512 | tf_op jit(solution)/shard_map/ppermute | solution.py:354
  4.3 1.6 %collective-permute-start.2 = (bf16[592,128]{1,0:T(8,128)(2,1)S(1)}, bf16[592,128]{1,0:T(8,128)(2,1)S(1)}, u32[]{:S(2)}, u32[]{:S(2)}) collective-permute-start(bf16[592,128]{1,0:T(8,128)(2,1)S(1)} %get-tuple-element.26), channel_id=1, source_target_pairs={{0,4},{2,6},{4,0},{6,2},{8,12},{10,14},{12,8},{14,10},{1,5},{3,7},... | collective-permute-start | bytes 454664 | tf_op jit(solution)/shard_map/ppermute | solution.py:354
  5.9 0.0 collective-permute-start.3
  5.9 0.0 copy-start.3
  5.9 1.9 %collective-permute-start.5 = (bf16[512,128]{1,0:T(8,128)(2,1)S(1)}, bf16[512,128]{1,0:T(8,128)(2,1)S(1)}, u32[]{:S(2)}, u32[]{:S(2)}) collective-permute-start(bf16[512,128]{1,0:T(8,128)(2,1)S(1)} %get-tuple-element.27.refs_5_.refs_4_), channel_id=1, source_target_pairs={{0,2},{2,0},{4,6},{6,4},{8,10},{10,8},{12,14},{14,12},{1,3},{3,1},... | collective-permute-start | bytes 393224 | tf_op jit(solution)/shard_map/ppermute | solution.py:354
  7.8 1.6 %collective-permute-start.6 = (bf16[512,128]{1,0:T(8,128)(2,1)S(1)}, bf16[512,128]{1,0:T(8,128)(2,1)S(1)}, u32[]{:S(2)}, u32[]{:S(2)}) collective-permute-start(bf16[512,128]{1,0:T(8,128)(2,1)S(1)} %get-tuple-element.27.refs_5_.refs_4_), channel_id=1, source_target_pairs={{0,4},{2,6},{4,0},{6,2},{8,12},{10,14},{12,8},{14,10},{1,5},{3,7},... | collective-permute-start | bytes 393224 | tf_op jit(solution)/shard_map/ppermute | solution.py:354
  9.4 0.0 collective-permute-done.1.refs_2_.refs_1_
  9.4 1.6 %collective-permute-start.7 = (bf16[512,128]{1,0:T(8,128)(2,1)S(1)}, bf16[512,128]{1,0:T(8,128)(2,1)S(1)}, u32[]{:S(2)}, u32[]{:S(2)}) collective-permute-start(bf16[512,128]{1,0:T(8,128)(2,1)S(1)} %get-tuple-element.27.refs_5_.refs_4_), channel_id=1, source_target_pairs={{0,6},{2,4},{4,2},{6,0},{8,14},{10,12},{12,10},{14,8},{1,7},{3,5},... | collective-permute-start | bytes 393224 | tf_op jit(solution)/shard_map/ppermute | solution.py:354
  11.0 0.0 copy-done.2
  11.0 0.0 copy-done.3
  11.0 0.0 copy-start.1
  11.1 0.1 copy.7.list_ref
  11.1 0.6 %copy-done.1 = s32[8]{0:T(128)S(1)} copy-done((s32[8]{0:T(128)S(1)}, s32[8]{0:T(128)}, u32[]{:S(2)}) %copy-start.1) | copy-done | bytes 56
  11.7 0.8 %shard_map.64 = (s32[1,2048]{1,0:T(1,128)S(1)}, bf16[256,2048]{1,0:T(8,128)(2,1)S(1)}, f32[8,128]{1,0:T(8,128)S(1)}) custom-call(s32[2,2048]{1,0:T(2,128)S(1)} %reshape.15.transition_ref, s32[8]{0:T(128)S(1)} %copy-done.1, s32[8,3]{1,0:T(8,128)S(1)} %copy.7.list_ref), custom_call_target="tpu_custom_call" | custom-call | flops 2097152 | bytes 1048576 | tf_op jit(solution)/shard_map/pallas_call | solution.py:27
  12.5 0.8 %collective-permute-done.3.refs_4_.refs_3_ = bf16[528,128]{1,0:T(8,128)(2,1)S(1)} collective-permute-done((bf16[528,128]{1,0:T(8,128)(2,1)S(1)}, bf16[528,128]{1,0:T(8,128)(2,1)S(1)}, u32[]{:S(2)}, u32[]{:S(2)}) %collective-permute-start.3) | collective-permute-done | bytes 135200 | tf_op jit(solution)/shard_map/ppermute | solution.py:354
  13.3 0.0 collective-permute-done.2.refs_3_.refs_2_
  13.3 0.3 shard_map.70
  13.6 2.9 %collective-permute-start.10 = (bf16[528,128]{1,0:T(8,128)(2,1)S(1)}, bf16[528,128]{1,0:T(8,128)(2,1)S(1)}, u32[]{:S(2)}, u32[]{:S(2)}) collective-permute-start(bf16[528,128]{1,0:T(8,128)(2,1)S(1)} %shard_map.70), channel_id=1, source_target_pairs={{0,8},{4,12},{8,0},{12,4},{1,9},{5,13},{9,1},{13,5},{2,10},{6,14},... | collective-permute-start | bytes 405512 | tf_op jit(solution)/shard_map/ppermute | solution.py:358
  16.6 2.0 %collective-permute-start = (bf16[64,128]{1,0:T(8,128)(2,1)S(1)}, bf16[64,128]{1,0:T(8,128)(2,1)S(1)}, u32[]{:S(2)}, u32[]{:S(2)}) collective-permute-start(bf16[64,128]{1,0:T(8,128)(2,1)S(1)} %get-tuple-element.24), channel_id=1, source_target_pairs={{0,4},{2,6},{4,0},{6,2},{8,12},{10,14},{12,8},{14,10},{1,5},{3,7},... | collective-permute-start | bytes 49160 | tf_op jit(solution)/shard_map/ppermute | solution.py:354
  18.5 2.9 %collective-permute-done.refs_0_ = bf16[64,128]{1,0:T(8,128)(2,1)S(1)} collective-permute-done((bf16[64,128]{1,0:T(8,128)(2,1)S(1)}, bf16[64,128]{1,0:T(8,128)(2,1)S(1)}, u32[]{:S(2)}, u32[]{:S(2)}) %collective-permute-start) | collective-permute-done | bytes 16416 | tf_op jit(solution)/shard_map/ppermute | solution.py:354
  21.5 0.3 shard_map.66.refs_0_
  21.8 0.1 collective-permute-start.4
  21.9 0.0 collective-permute-done.5.refs_6_.refs_5_
  21.9 0.0 collective-permute-done.6.refs_7_.refs_6_
  21.9 0.0 collective-permute-done.7.refs_8_.refs_7_
  21.9 0.3 shard_map.69
  22.2 2.7 %collective-permute-start.9 = (bf16[512,128]{1,0:T(8,128)(2,1)S(1)}, bf16[512,128]{1,0:T(8,128)(2,1)S(1)}, u32[]{:S(2)}, u32[]{:S(2)}) collective-permute-start(bf16[512,128]{1,0:T(8,128)(2,1)S(1)} %shard_map.69), channel_id=1, source_target_pairs={{0,8},{4,12},{8,0},{12,4},{1,9},{5,13},{9,1},{13,5},{2,10},{6,14},... | collective-permute-start | bytes 393224 | tf_op jit(solution)/shard_map/ppermute | solution.py:358
  24.9 0.3 shard_map.67.refs_2_
  25.2 0.3 collective-permute-start.8
  25.4 0.0 collective-permute-done.10.refs_0_
  25.4 0.3 collective-permute-start.11
  25.7 6.1 %collective-permute-done.9.refs_0_ = bf16[512,128]{1,0:T(8,128)(2,1)S(1)} collective-permute-done((bf16[512,128]{1,0:T(8,128)(2,1)S(1)}, bf16[512,128]{1,0:T(8,128)(2,1)S(1)}, u32[]{:S(2)}, u32[]{:S(2)}) %collective-permute-start.9) | collective-permute-done | bytes 131104 | tf_op jit(solution)/shard_map/ppermute | solution.py:358
  31.9 0.0 collective-permute-start.12
  31.9 0.0 collective-permute-done.8.refs_3_
  31.9 0.0 collective-permute-done.4.refs_1_
  31.9 1.4 %shard_map.68 = (f32[64,2048]{1,0:T(8,128)S(1)}, f32[1,2048]{1,0:T(1,128)S(1)}) custom-call(s32[1,2048]{1,0:T(1,128)S(1)} %get-tuple-element.20.where_ref, bf16[256,2048]{1,0:T(8,128)(2,1)S(1)} %get-tuple-element.21.onehot_ref, bf16[528,128]{1,0:T(8,128)(2,1)S(1)} %shard_map.66.refs_0_, bf16[528,128]{1,0:T(8,128)(2,1)S(1)} %collective-permute-done.4.refs_1_, ...), custom_call_target="tpu_custom_call" | custom-call | flops 1073741824 | bytes 524288 | tf_op jit(solution)/shard_map/pallas_call | solution.py:27
  33.3 0.0 copy-start
  33.3 0.0 collective-permute-done.11.refs_1_
  33.3 0.8 %shard_map.71 = (f32[64,2048]{1,0:T(8,128)S(1)}, f32[1,2048]{1,0:T(1,128)S(1)}) custom-call(s32[1,2048]{1,0:T(1,128)S(1)} %get-tuple-element.20.where_ref, bf16[256,2048]{1,0:T(8,128)(2,1)S(1)} %get-tuple-element.21.onehot_ref, bf16[528,128]{1,0:T(8,128)(2,1)S(1)} %collective-permute-done.10.refs_0_, bf16[528,128]{1,0:T(8,128)(2,1)S(1)} %collective-permute-done.11.refs_1_), custom_call_target="tpu_custom_call" | custom-call | flops 536870912 | bytes 524288 | tf_op jit(solution)/shard_map/pallas_call | solution.py:27
  34.2 0.2 copy-done
  34.3 0.5 %shard_map.72 = (f32[64,2048]{1,0:T(8,128)S(1)}, f32[64,2048]{1,0:T(8,128)S(1)}, f32[1,2048]{1,0:T(1,128)S(1)}) custom-call(f32[64,2048]{1,0:T(8,128)S(1)} %bitcast.4, s32[1,2048]{1,0:T(1,128)S(1)} %get-tuple-element.20.where_ref, bf16[256,2048]{1,0:T(8,128)(2,1)S(1)} %get-tuple-element.21.onehot_ref, f32[64,2048]{1,0:T(8,128)S(1)} %get-tuple-element.28.own_ref, ...), custom_call_target="tpu_custom_call" | custom-call | flops 268435456 | bytes 2097152 | tf_op jit(solution)/shard_map/pallas_call | solution.py:27
  34.8 0.0 collective-permute-done.12.refs_1_
  34.8 1.2 %finish.1 = f32[64,2048]{1,0:T(8,128)} custom-call(s32[1,2048]{1,0:T(1,128)S(1)} %get-tuple-element.20.where_ref, bf16[256,2048]{1,0:T(8,128)(2,1)S(1)} %get-tuple-element.21.onehot_ref, f32[64,2048]{1,0:T(8,128)S(1)} %get-tuple-element.32.known_ref, f32[64,2048]{1,0:T(8,128)S(1)} %get-tuple-element.33.base_ref, f32[1,2048]{1,0:T(1,128)S(1)} %get-tuple-element.34.refs_0_, ...), custom_call_target="tpu_custom_call" | custom-call | flops 268435456 | bytes 1572864 | tf_op jit(solution)/shard_map/finish/pallas_call | solution.py:322
  (1 shorter events, 0.0 us)
Async XLA Ops:
  0.0 11.0 %copy-start.2 = (s32[4096]{0:T(1024)S(1)}, s32[4096]{0:T(1024)}, u32[]{:S(2)}) copy-start(s32[4096]{0:T(1024)} %param.11) | copy-start | bytes 49156
  1.3 8.1 %collective-permute-start.1 = (bf16[528,128]{1,0:T(8,128)(2,1)S(1)}, bf16[528,128]{1,0:T(8,128)(2,1)S(1)}, u32[]{:S(2)}, u32[]{:S(2)}) collective-permute-start(bf16[528,128]{1,0:T(8,128)(2,1)S(1)} %get-tuple-element.25.refs_1_.refs_0_), channel_id=1, source_target_pairs={{0,2},{2,0},{4,6},{6,4},{8,10},{10,8},{12,14},{14,12},{1,3},{3,1},... | collective-permute-start | bytes 405512 | tf_op jit(solution)/shard_map/ppermute | solution.py:354
  4.3 9.0 %collective-permute-start.2 = (bf16[592,128]{1,0:T(8,128)(2,1)S(1)}, bf16[592,128]{1,0:T(8,128)(2,1)S(1)}, u32[]{:S(2)}, u32[]{:S(2)}) collective-permute-start(bf16[592,128]{1,0:T(8,128)(2,1)S(1)} %get-tuple-element.26), channel_id=1, source_target_pairs={{0,4},{2,6},{4,0},{6,2},{8,12},{10,14},{12,8},{14,10},{1,5},{3,7},... | collective-permute-start | bytes 454664 | tf_op jit(solution)/shard_map/ppermute | solution.py:354
  5.9 7.4 %collective-permute-start.3 = (bf16[528,128]{1,0:T(8,128)(2,1)S(1)}, bf16[528,128]{1,0:T(8,128)(2,1)S(1)}, u32[]{:S(2)}, u32[]{:S(2)}) collective-permute-start(bf16[528,128]{1,0:T(8,128)(2,1)S(1)} %get-tuple-element.25.refs_1_.refs_0_), channel_id=1, source_target_pairs={{0,6},{2,4},{4,2},{6,0},{8,14},{10,12},{12,10},{14,8},{1,7},{3,5},... | collective-permute-start | bytes 405512 | tf_op jit(solution)/shard_map/ppermute | solution.py:354
  5.9 5.1 %copy-start.3 = (s32[8,3]{0,1:T(4,128)S(1)}, s32[8,3]{0,1:T(4,128)}, u32[]{:S(2)}) copy-start(s32[8,3]{0,1:T(4,128)} %param.9) | copy-start | bytes 292
  5.9 16.0 %collective-permute-start.5 = (bf16[512,128]{1,0:T(8,128)(2,1)S(1)}, bf16[512,128]{1,0:T(8,128)(2,1)S(1)}, u32[]{:S(2)}, u32[]{:S(2)}) collective-permute-start(bf16[512,128]{1,0:T(8,128)(2,1)S(1)} %get-tuple-element.27.refs_5_.refs_4_), channel_id=1, source_target_pairs={{0,2},{2,0},{4,6},{6,4},{8,10},{10,8},{12,14},{14,12},{1,3},{3,1},... | collective-permute-start | bytes 393224 | tf_op jit(solution)/shard_map/ppermute | solution.py:354
  7.8 14.1 %collective-permute-start.6 = (bf16[512,128]{1,0:T(8,128)(2,1)S(1)}, bf16[512,128]{1,0:T(8,128)(2,1)S(1)}, u32[]{:S(2)}, u32[]{:S(2)}) collective-permute-start(bf16[512,128]{1,0:T(8,128)(2,1)S(1)} %get-tuple-element.27.refs_5_.refs_4_), channel_id=1, source_target_pairs={{0,4},{2,6},{4,0},{6,2},{8,12},{10,14},{12,8},{14,10},{1,5},{3,7},... | collective-permute-start | bytes 393224 | tf_op jit(solution)/shard_map/ppermute | solution.py:354
  9.4 12.5 %collective-permute-start.7 = (bf16[512,128]{1,0:T(8,128)(2,1)S(1)}, bf16[512,128]{1,0:T(8,128)(2,1)S(1)}, u32[]{:S(2)}, u32[]{:S(2)}) collective-permute-start(bf16[512,128]{1,0:T(8,128)(2,1)S(1)} %get-tuple-element.27.refs_5_.refs_4_), channel_id=1, source_target_pairs={{0,6},{2,4},{4,2},{6,0},{8,14},{10,12},{12,10},{14,8},{1,7},{3,5},... | collective-permute-start | bytes 393224 | tf_op jit(solution)/shard_map/ppermute | solution.py:354
  11.0 0.7 %copy-start.1 = (s32[8]{0:T(128)S(1)}, s32[8]{0:T(128)}, u32[]{:S(2)}) copy-start(s32[8]{0:T(128)} %count_ref.1) | copy-start | bytes 100
  13.6 11.8 %collective-permute-start.10 = (bf16[528,128]{1,0:T(8,128)(2,1)S(1)}, bf16[528,128]{1,0:T(8,128)(2,1)S(1)}, u32[]{:S(2)}, u32[]{:S(2)}) collective-permute-start(bf16[528,128]{1,0:T(8,128)(2,1)S(1)} %shard_map.70), channel_id=1, source_target_pairs={{0,8},{4,12},{8,0},{12,4},{1,9},{5,13},{9,1},{13,5},{2,10},{6,14},... | collective-permute-start | bytes 405512 | tf_op jit(solution)/shard_map/ppermute | solution.py:358
  16.6 4.9 %collective-permute-start = (bf16[64,128]{1,0:T(8,128)(2,1)S(1)}, bf16[64,128]{1,0:T(8,128)(2,1)S(1)}, u32[]{:S(2)}, u32[]{:S(2)}) collective-permute-start(bf16[64,128]{1,0:T(8,128)(2,1)S(1)} %get-tuple-element.24), channel_id=1, source_target_pairs={{0,4},{2,6},{4,0},{6,2},{8,12},{10,14},{12,8},{14,10},{1,5},{3,7},... | collective-permute-start | bytes 49160 | tf_op jit(solution)/shard_map/ppermute | solution.py:354
  21.8 10.1 %collective-permute-start.4 = (bf16[528,128]{1,0:T(8,128)(2,1)S(1)}, bf16[528,128]{1,0:T(8,128)(2,1)S(1)}, u32[]{:S(2)}, u32[]{:S(2)}) collective-permute-start(bf16[528,128]{1,0:T(8,128)(2,1)S(1)} %shard_map.66.refs_0_), channel_id=1, source_target_pairs={{0,1},{1,0},{2,3},{3,2},{4,5},{5,4},{6,7},{7,6},{8,9},{9,8},{10,11... | collective-permute-start | bytes 405512 | tf_op jit(solution)/shard_map/ppermute | solution.py:362
  22.2 9.7 %collective-permute-start.9 = (bf16[512,128]{1,0:T(8,128)(2,1)S(1)}, bf16[512,128]{1,0:T(8,128)(2,1)S(1)}, u32[]{:S(2)}, u32[]{:S(2)}) collective-permute-start(bf16[512,128]{1,0:T(8,128)(2,1)S(1)} %shard_map.69), channel_id=1, source_target_pairs={{0,8},{4,12},{8,0},{12,4},{1,9},{5,13},{9,1},{13,5},{2,10},{6,14},... | collective-permute-start | bytes 393224 | tf_op jit(solution)/shard_map/ppermute | solution.py:358
  25.2 6.7 %collective-permute-start.8 = (bf16[512,128]{1,0:T(8,128)(2,1)S(1)}, bf16[512,128]{1,0:T(8,128)(2,1)S(1)}, u32[]{:S(2)}, u32[]{:S(2)}) collective-permute-start(bf16[512,128]{1,0:T(8,128)(2,1)S(1)} %shard_map.67.refs_2_), channel_id=1, source_target_pairs={{0,1},{1,0},{2,3},{3,2},{4,5},{5,4},{6,7},{7,6},{8,9},{9,8},{10,11... | collective-permute-start | bytes 393224 | tf_op jit(solution)/shard_map/ppermute | solution.py:362
  25.4 7.9 %collective-permute-start.11 = (bf16[528,128]{1,0:T(8,128)(2,1)S(1)}, bf16[528,128]{1,0:T(8,128)(2,1)S(1)}, u32[]{:S(2)}, u32[]{:S(2)}) collective-permute-start(bf16[528,128]{1,0:T(8,128)(2,1)S(1)} %collective-permute-done.10.refs_0_), channel_id=1, source_target_pairs={{0,1},{1,0},{2,3},{3,2},{4,5},{5,4},{6,7},{7,6},{8,9},{9,8},{10,11... | collective-permute-start | bytes 405512 | tf_op jit(solution)/shard_map/ppermute | solution.py:362
  31.9 3.0 %collective-permute-start.12 = (bf16[512,128]{1,0:T(8,128)(2,1)S(1)}, bf16[512,128]{1,0:T(8,128)(2,1)S(1)}, u32[]{:S(2)}, u32[]{:S(2)}) collective-permute-start(bf16[512,128]{1,0:T(8,128)(2,1)S(1)} %collective-permute-done.9.refs_0_), channel_id=1, source_target_pairs={{0,1},{1,0},{2,3},{3,2},{4,5},{5,4},{6,7},{7,6},{8,9},{9,8},{10,11... | collective-permute-start | bytes 393224 | tf_op jit(solution)/shard_map/ppermute | solution.py:362
  33.3 1.0 %copy-start = (f32[1,1,64,2048]{3,2,1,0:T(8,128)S(1)}, f32[1,1,64,2048]{3,2,1,0:T(8,128)}, u32[]{:S(2)}) copy-start(f32[1,1,64,2048]{3,2,1,0:T(8,128)} %param.7) | copy-start | bytes 1572868
